TPU v7x, 128 devices: a whole 4x4x4 slice. The times are simulated.
128 devices in a mesh: gz: 8 (over x, core), xy: 16 (over y, z).
Axes of the slice: x: 4, y: 4, z: 4, core: 2. Of those that a mesh axis runs over, the one named last changes fastest.
Arguments:
- parent_feat: bfloat16 [128, 64, 2048], P(('gz', 'xy')), may hold values from -6 to 6
- parent_cell: int32 [128, 2048], P(('gz', 'xy')), may hold values from 0 to 255
- send_count: int32 [128, 128], P(('gz', 'xy')), may hold values from 1 to 16, as said below
- up_weight: bfloat16 [8, 64, 64], replicated, may hold values from -0.75 to 0.75
- conv_one: bfloat16 [27, 64, 64], replicated, may hold values from -0.15625 to 0.15625
- conv_two: bfloat16 [27, 64, 64], replicated, may hold values from -0.15625 to 0.15625
- child_mask: int32 [32, 8, 1024], P('xy', None, 'gz'), may hold values 0 or 1
- cotangent: bfloat16 [64, 32, 8, 1024], P(None, 'xy', None, 'gz'), may hold values from -6 to 6
Outputs:
- decoded: bfloat16 [64, 32, 8, 1024], P(None, 'xy', None, 'gz')
- grad_parent: bfloat16 [128, 64, 2048], P(('gz', 'xy'))
- grad_one: float32 [27, 64, 64], replicated
- grad_two: float32 [27, 64, 64], replicated
- grad_up: float32 [8, 64, 64], replicated
Inputs may be any that keep to these rules, and one draw needn't show every extreme that they name: `send_count`: some receiver gets 16 live slots from every sender, and every sender fills all 16 slots to some receiver. `parent_cell`: several slots may name the same parent voxel; their features add.
All inputs are finite; a program needn't handle non-finite values. No bound on the sum of `child_mask` on one device may be relied on, other than what follows from the above.
Results may differ from a plain program's by a relative error of at most 0.008.
Values may be sent and summed in bfloat16 or wider, within the bound.
No kernel may reach another device: no remote copies, remote signals or barrier semaphores. Data moves between devices by JAX's collectives and lax.ppermute only.
A program may use at most 64 MiB of HBM per device.

v0:
```python
import math
import jax
import jax.numpy as jnp
from jax import lax
from jax.sharding import PartitionSpec as P

OFFSETS = [(a, b, c) for a in (-1, 0, 1) for b in (-1, 0, 1) for c in (-1, 0, 1)]


def with_halo(shard, sides, width):
    for axis, dim in sides:
        devices, length = (lax.axis_size(axis), shard.shape[dim])
        up = [(i, (i + 1) % devices) for i in range(devices - 1)]
        down = [(j, i) for i, j in up]
        last = lax.slice_in_dim(shard, length - width, length, axis=dim)
        first = lax.slice_in_dim(shard, 0, width, axis=dim)
        before = lax.ppermute(last, axis, up)
        after = lax.ppermute(first, axis, down)
        shard = jnp.concatenate([before, shard, after], axis=dim)
    return shard


def extend(field):
    bordered = with_halo(field, (("xy", 1), ("gz", 3)), 1)
    return jnp.pad(bordered, ((0, 0), (0, 0), (1, 1), (0, 0)))


def window(padded, offset, direction, shape):
    nx, ny, nz = (shape[1], shape[2], shape[3])
    ox, oy, oz = (offset[0] * direction, offset[1] * direction, offset[2] * direction)
    part = padded[:, 1 + ox : 1 + ox + nx, 1 + oy : 1 + oy + ny, 1 + oz : 1 + oz + nz]
    return part.reshape(shape[0], -1)


def orient(matrix, direction):
    return matrix if direction > 0 else matrix.T


def convolve(padded, weights, direction, shape):
    total = jnp.zeros((shape[0], shape[1] * shape[2] * shape[3]), jnp.float32)
    for index, offset in enumerate(OFFSETS):
        total = total + jnp.dot(
            orient(weights[index], direction),
            window(padded, offset, direction, shape),
            preferred_element_type=jnp.float32,
        )
    return total.reshape(shape)


def weight_terms(delta, padded, shape):
    flat = delta.reshape(shape[0], -1)
    terms = [
        lax.dot_general(
            flat,
            window(padded, offset, 1, shape),
            (((1,), (1,)), ((), ())),
            preferred_element_type=jnp.float32,
        )
        for offset in OFFSETS
    ]
    return jnp.stack(terms)


def silu_slope(value):
    sig = jax.nn.sigmoid(value)
    return sig * (1.0 + value * (1.0 - sig))


def local(
    parent_feat, parent_cell, send_count, up_weight, conv_one, conv_two, child_mask, cotangent
):
    channels, size_x, size_y, size_z = cotangent.shape
    shape = cotangent.shape
    count_gz = lax.axis_size("gz")
    count_xy = lax.axis_size("xy")
    devices_all = count_gz * count_xy
    slot_total = parent_feat.shape[2]
    capacity = slot_total // devices_all
    half_x, half_y, half_z = (size_x // 2, size_y // 2, size_z // 2)
    parent_total = half_x * half_y * half_z
    slot_pos = jnp.arange(slot_total, dtype=jnp.int32) % capacity
    live = slot_pos < jnp.repeat(send_count[0], capacity)
    feats = jnp.where(live[None, :], parent_feat[0], jnp.zeros_like(parent_feat[0]))
    got_feat, got_cell = (
        lax.all_to_all(feats, ("gz", "xy"), split_axis=1, concat_axis=1, tiled=True),
        lax.all_to_all(parent_cell, ("gz", "xy"), split_axis=1, concat_axis=1, tiled=True),
    )
    got_cell = got_cell.reshape(slot_total)
    onehot = (got_cell[:, None] == jnp.arange(parent_total, dtype=jnp.int32)[None, :]).astype(
        jnp.bfloat16
    )
    parent_grid = jnp.dot(got_feat, onehot, preferred_element_type=jnp.float32).astype(jnp.bfloat16)
    up8 = jnp.einsum("ocd,dq->ocq", up_weight, parent_grid, preferred_element_type=jnp.float32)
    up = (
        up8.reshape(2, 2, 2, channels, half_x, half_y, half_z)
        .transpose(3, 4, 0, 5, 1, 6, 2)
        .reshape(shape)
    )
    maskf = child_mask.astype(jnp.float32)
    lifted = (maskf * up).astype(jnp.bfloat16)
    lifted_pad = extend(lifted)
    first_pre = convolve(lifted_pad, conv_one, 1, shape)
    first_act = (maskf * jax.nn.silu(first_pre)).astype(jnp.bfloat16)
    first_pad = extend(first_act)
    second_pre = convolve(first_pad, conv_two, 1, shape)
    decoded = (maskf * jax.nn.silu(second_pre)).astype(jnp.bfloat16)
    delta_two = (cotangent.astype(jnp.float32) * maskf * silu_slope(second_pre)).astype(
        jnp.bfloat16
    )
    term_two = weight_terms(delta_two, first_pad, shape)
    back_one = convolve(extend(delta_two), conv_two, -1, shape)
    delta_one = (back_one * maskf * silu_slope(first_pre)).astype(jnp.bfloat16)
    term_one = weight_terms(delta_one, lifted_pad, shape)
    delta_up = (convolve(extend(delta_one), conv_one, -1, shape) * maskf).astype(jnp.bfloat16)
    du8 = (
        delta_up.reshape(channels, half_x, 2, half_y, 2, half_z, 2)
        .transpose(2, 4, 6, 0, 1, 3, 5)
        .reshape(8, channels, parent_total)
    )
    term_up = jnp.einsum("ocq,dq->ocd", du8, parent_grid, preferred_element_type=jnp.float32)
    delta_parent = jnp.einsum(
        "ocd,ocq->dq", up_weight, du8, preferred_element_type=jnp.float32
    ).astype(jnp.bfloat16)
    slot_grad = lax.dot_general(
        delta_parent, onehot, (((1,), (1,)), ((), ())), preferred_element_type=jnp.float32
    ).astype(jnp.bfloat16)
    returned = lax.all_to_all(slot_grad, ("gz", "xy"), split_axis=1, concat_axis=1, tiled=True)
    grad_parent = jnp.where(live[None, :], returned, jnp.zeros_like(returned))[None]
    sum_one, sum_two, sum_up = lax.psum((term_one, term_two, term_up), ("gz", "xy"))
    scale = 1.0 / math.sqrt(size_x * count_xy * size_y * size_z * count_gz)
    return (decoded, grad_parent, sum_one * scale, sum_two * scale, sum_up * scale)


def solution(mesh):
    placed = (
        P(("gz", "xy"), None, None),
        P(("gz", "xy"), None),
        P(("gz", "xy"), None),
        P(),
        P(),
        P(),
        P("xy", None, "gz"),
        P(None, "xy", None, "gz"),
    )
    return jax.shard_map(
        local,
        mesh=mesh,
        in_specs=placed,
        out_specs=(P(None, "xy", None, "gz"), P(("gz", "xy"), None, None), P(), P(), P()),
        check_vma=False,
    )
```

profile of v0, /device:TPU:1, one launch (start us, length us, event | category | flops | bytes accessed | tf_op | source)
XLA Modules:
  0.0 432.3 jit_solution(10108309760339999828)
XLA Ops:
  7.7 1.4 reduce.6
  9.8 11.5 %all-to-all-start.1 = ((s32[1,128,16]{2,0,1:T(1,128)}), s32[1,128,16]{2,0,1:T(1,128)S(1)}, u32[]{:S(2)}, u32[]{:S(2)}) async-start(s32[1,128,16]{2,0,1:T(1,128)} %bitcast.3), calls=%async_computation.1 | async-start | bytes 131072 | tf_op jit(solution)/shard_map/all_to_all | solution.py:86
  22.0 1.2 copy.273
  24.6 6.2 %all-to-all-done.1 = s32[1,128,16]{2,0,1:T(1,128)S(1)} async-done(((s32[1,128,16]{2,0,1:T(1,128)}), s32[1,128,16]{2,0,1:T(1,128)S(1)}, u32[]{:S(2)}, u32[]{:S(2)}) %all-to-all-start.1) | async-done | bytes 8224 | tf_op jit(solution)/shard_map/all_to_all | solution.py:86
  30.8 4.5 %all-to-all-start = ((bf16[128,2,512]{2,1,0:T(2,128)(2,1)}), bf16[128,2,512]{2,1,0:T(2,128)(2,1)S(1)}, u32[]{:S(2)}, u32[]{:S(2)}) async-start(bf16[128,2,512]{2,1,0:T(2,128)(2,1)} %reshape.685), calls=%async_computation | async-start | bytes 524288 | tf_op jit(solution)/shard_map/all_to_all | solution.py:85
  36.8 9.8 %all-to-all-done = bf16[128,2,512]{2,1,0:T(2,128)(2,1)S(1)} async-done(((bf16[128,2,512]{2,1,0:T(2,128)(2,1)}), bf16[128,2,512]{2,1,0:T(2,128)(2,1)S(1)}, u32[]{:S(2)}, u32[]{:S(2)}) %all-to-all-start) | async-done | bytes 262176 | tf_op jit(solution)/shard_map/all_to_all | solution.py:85
  49.3 2.5 collective-permute-start
  51.8 1.3 collective-permute-start.1
  53.9 3.6 collective-permute-done.1
  57.8 4.3 collective-permute-start.2
  62.1 1.9 collective-permute-start.3
  64.0 1.7 fusion.118
  65.7 2.5 collective-permute-done.2
  68.2 4.4 %collective-permute-done.3 = bf16[64,4,8,1]{3,0,2,1:T(8,128)(2,1)S(1)} collective-permute-done((bf16[64,4,8,1]{3,0,2,1:T(8,128)(2,1)S(1)}, bf16[64,4,8,1]{3,0,2,1:T(8,128)(2,1)S(1)}, u32[]{:S(2)}, u32[]{:S(2)}) %collective-permute-start.3) | collective-permute-done | bytes 4128 | tf_op jit(solution)/shard_map/ppermute | solution.py:18
  73.2 1.2 fusion.605
  92.9 2.0 collective-permute-start.4
  94.9 1.3 collective-permute-start.5
  96.8 3.8 collective-permute-done.5
  101.4 1.2 fusion.608
  102.5 4.1 collective-permute-start.6
  106.7 2.5 collective-permute-start.7
  110.8 2.3 collective-permute-done.6
  113.1 4.4 %collective-permute-done.7 = bf16[64,4,8,1]{3,0,2,1:T(8,128)(2,1)} collective-permute-done((bf16[64,4,8,1]{3,0,2,1:T(8,128)(2,1)}, bf16[64,4,8,1]{3,0,2,1:T(8,128)(2,1)}, u32[]{:S(2)}, u32[]{:S(2)}) %collective-permute-start.7) | collective-permute-done | bytes 4128 | tf_op jit(solution)/shard_map/ppermute | solution.py:18
  117.5 1.9 select_maximum_fusion.8
  119.4 1.2 fusion.604
  121.6 1.5 pad_maximum_fusion.36
  123.3 1.7 pad_maximum_fusion.35
  141.8 1.2 multiply_convert_fusion.2
  149.3 5.2 %collective-permute-start.8 = (bf16[64,1,8,128]{3,0,2,1:T(8,128)(2,1)S(1)}, bf16[64,1,8,128]{3,0,2,1:T(8,128)(2,1)S(1)}, u32[]{:S(2)}, u32[]{:S(2)}) collective-permute-start(bf16[64,1,8,128]{3,0,2,1:T(8,128)(2,1)S(1)} %get-tuple-element.144), channel_id=1, source_target_pairs={{0,1},{1,2},{2,3},{3,4},{4,5},{5,6},{6,7},{7,8},{8,9},{9,10},{10,1... | collective-permute-start | bytes 393224 | tf_op jit(solution)/shard_map/ppermute | solution.py:17
  154.5 1.3 collective-permute-start.9
  156.4 3.8 collective-permute-done.9
  160.6 3.8 collective-permute-start.10
  164.4 1.9 collective-permute-start.11
  166.8 3.7 collective-permute-done.10
  170.5 4.4 %collective-permute-done.11 = bf16[64,4,8,1]{3,0,2,1:T(8,128)(2,1)S(1)} collective-permute-done((bf16[64,4,8,1]{3,0,2,1:T(8,128)(2,1)S(1)}, bf16[64,4,8,1]{3,0,2,1:T(8,128)(2,1)S(1)}, u32[]{:S(2)}, u32[]{:S(2)}) %collective-permute-start.11) | collective-permute-done | bytes 4128 | tf_op jit(solution)/shard_map/ppermute | solution.py:18
  175.5 1.3 fusion.603
  184.1 1.0 convolution_bitcast_fusion.31
  185.3 1.0 convolution_bitcast_fusion.32
  186.5 1.0 convolution_bitcast_fusion.36
  188.8 1.0 convolution_bitcast_fusion.38
  190.0 1.0 convolution_bitcast_fusion.39
  195.3 1.0 multiply_convert_fusion.1
  203.5 3.5 collective-permute-start.12
  207.0 1.3 collective-permute-start.13
  208.9 3.8 collective-permute-done.13
  213.0 4.1 collective-permute-start.14
  217.2 1.9 collective-permute-start.15
  219.4 3.9 collective-permute-done.14
  223.3 4.4 %collective-permute-done.15 = bf16[64,4,8,1]{3,0,2,1:T(8,128)(2,1)S(1)} collective-permute-done((bf16[64,4,8,1]{3,0,2,1:T(8,128)(2,1)S(1)}, bf16[64,4,8,1]{3,0,2,1:T(8,128)(2,1)S(1)}, u32[]{:S(2)}, u32[]{:S(2)}) %collective-permute-start.15) | collective-permute-done | bytes 4128 | tf_op jit(solution)/shard_map/ppermute | solution.py:18
  228.4 1.1 fusion.602
  238.1 1.0 convolution_bitcast_fusion.24
  239.2 1.0 convolution_bitcast_fusion.20
  240.4 1.0 convolution_bitcast_fusion.21
  241.6 1.0 convolution_bitcast_fusion.22
  242.8 1.0 convolution_bitcast_fusion.26
  243.9 1.0 convolution_bitcast_fusion.27
  246.3 1.0 convolution_bitcast_fusion.29
  249.6 1.4 fusion.121
  252.7 1.0 reshape.687
  253.7 7.1 %all-to-all-start.2 = ((bf16[128,2,512]{2,1,0:T(2,128)(2,1)}), bf16[128,2,512]{2,1,0:T(2,128)(2,1)S(1)}, u32[]{:S(2)}, u32[]{:S(2)}) async-start(bf16[128,2,512]{2,1,0:T(2,128)(2,1)} %reshape.687), calls=%async_computation.2 | async-start | bytes 524288 | tf_op jit(solution)/shard_map/all_to_all | solution.py:127
  262.7 9.3 %all-to-all-done.2 = bf16[128,2,512]{2,1,0:T(2,128)(2,1)S(1)} async-done(((bf16[128,2,512]{2,1,0:T(2,128)(2,1)}), bf16[128,2,512]{2,1,0:T(2,128)(2,1)S(1)}, u32[]{:S(2)}, u32[]{:S(2)}) %all-to-all-start.2) | async-done | bytes 262176 | tf_op jit(solution)/shard_map/all_to_all | solution.py:127
  273.6 147.1 %all-reduce.7.cloned.1.call-done = (f32[27,64,64]{2,1,0:T(8,128)}, f32[27,64,64]{2,1,0:T(8,128)}, f32[8,64,64]{2,1,0:T(8,128)}) async-done(((f32[27,64,64]{2,1,0:T(8,128)}, f32[27,64,64]{2,1,0:T(8,128)}, f32[8,64,64]{2,1,0:T(8,128)}), (f32[27,64,64]{2,1,0:T(8,128)}, f32[27,64,64]{2,1,0:T(8,128)}, f32[8,64,64]{2,1,0:T(8,128)})) %all-reduce.7.cloned.1.call-update) | async-done | bytes 1015824 | tf_op jit(solution)/shard_map/psum | solution.py:129
  420.7 1.7 broadcast_multiply_fusion.2
  422.4 2.9 broadcast_multiply_fusion
  (389 shorter events, 96.2 us)
Async XLA Ops:
  7.2 40.4 %copy-start = (bf16[8,64,64]{2,1,0:T(8,128)(2,1)S(1)}, bf16[8,64,64]{2,1,0:T(8,128)(2,1)}, u32[]{:S(2)}) copy-start(bf16[8,64,64]{2,1,0:T(8,128)(2,1)} %param.11) | copy-start | bytes 196612
  9.8 21.0 %all-to-all-start.1 = ((s32[1,128,16]{2,0,1:T(1,128)}), s32[1,128,16]{2,0,1:T(1,128)S(1)}, u32[]{:S(2)}, u32[]{:S(2)}) async-start(s32[1,128,16]{2,0,1:T(1,128)} %bitcast.3), calls=%async_computation.1 | async-start | bytes 131072 | tf_op jit(solution)/shard_map/all_to_all | solution.py:86
  23.2 12.0 %copy-start.33 = (s32[2,8,128]{2,1,0:T(8,128)S(1)}, s32[2,8,128]{2,1,0:T(8,128)}, u32[]{:S(2)}) copy-start(s32[2,8,128]{2,1,0:T(8,128)} %param.14) | copy-start | bytes 24580
  30.8 15.7 %all-to-all-start = ((bf16[128,2,512]{2,1,0:T(2,128)(2,1)}), bf16[128,2,512]{2,1,0:T(2,128)(2,1)S(1)}, u32[]{:S(2)}, u32[]{:S(2)}) async-start(bf16[128,2,512]{2,1,0:T(2,128)(2,1)} %reshape.685), calls=%async_computation | async-start | bytes 524288 | tf_op jit(solution)/shard_map/all_to_all | solution.py:85
  36.8 10.1 %copy-start.34 = (s32[2048]{0:T(1024)}, s32[2048]{0:T(1024)S(1)}, u32[]{:S(2)}) copy-start(s32[2048]{0:T(1024)S(1)} %eq.17) | copy-start | bytes 24580
  47.6 1.3 copy-start.30
  49.3 4.6 %collective-permute-start = (bf16[64,1,8,128]{3,0,2,1:T(8,128)(2,1)S(1)}, bf16[64,1,8,128]{3,0,2,1:T(8,128)(2,1)S(1)}, u32[]{:S(2)}, u32[]{:S(2)}) collective-permute-start(bf16[64,1,8,128]{3,0,2,1:T(8,128)(2,1)S(1)} %get-tuple-element.148), channel_id=1, source_target_pairs={{0,1},{1,2},{2,3},{3,4},{4,5},{5,6},{6,7},{7,8},{8,9},{9,10},{10,1... | collective-permute-start | bytes 393224 | tf_op jit(solution)/shard_map/ppermute | solution.py:17
  51.8 5.7 %collective-permute-start.1 = (bf16[64,1,8,128]{3,0,2,1:T(8,128)(2,1)S(1)}, bf16[64,1,8,128]{3,0,2,1:T(8,128)(2,1)S(1)}, u32[]{:S(2)}, u32[]{:S(2)}) collective-permute-start(bf16[64,1,8,128]{3,0,2,1:T(8,128)(2,1)S(1)} %get-tuple-element.149), channel_id=1, source_target_pairs={{1,0},{2,1},{3,2},{4,3},{5,4},{6,5},{7,6},{8,7},{9,8},{10,9},{11,1... | collective-permute-start | bytes 393224 | tf_op jit(solution)/shard_map/ppermute | solution.py:18
  53.6 10.4 %copy-start.1 = (f32[2,4,2,64,2]{4,3,2,1,0:T(8,128)}, f32[2,4,2,64,2]{4,3,2,1,0:T(8,128)S(1)}, u32[]{:S(2)}) copy-start(f32[2,4,2,64,2]{4,3,2,1,0:T(8,128)S(1)} %mul.119) | copy-start | bytes 24580
  53.9 18.7 %copy-start.17 = (bf16[64,1,8,128]{3,0,2,1:T(8,128)(2,1)}, bf16[64,1,8,128]{3,0,2,1:T(8,128)(2,1)S(1)}, u32[]{:S(2)}) copy-start(bf16[64,1,8,128]{3,0,2,1:T(8,128)(2,1)S(1)} %collective-permute-done) | copy-start | bytes 393220
  57.8 10.4 %collective-permute-start.2 = (bf16[64,4,8,1]{3,0,2,1:T(8,128)(2,1)S(1)}, bf16[64,4,8,1]{3,0,2,1:T(8,128)(2,1)S(1)}, u32[]{:S(2)}, u32[]{:S(2)}) collective-permute-start(bf16[64,4,8,1]{3,0,2,1:T(8,128)(2,1)S(1)} %get-tuple-element.132), channel_id=1, source_target_pairs={{0,16},{16,32},{32,48},{48,64},{64,80},{80,96},{96,112},{1,17},{17... | collective-permute-start | bytes 12296 | tf_op jit(solution)/shard_map/ppermute | solution.py:17
  62.1 10.5 %collective-permute-start.3 = (bf16[64,4,8,1]{3,0,2,1:T(8,128)(2,1)S(1)}, bf16[64,4,8,1]{3,0,2,1:T(8,128)(2,1)S(1)}, u32[]{:S(2)}, u32[]{:S(2)}) collective-permute-start(bf16[64,4,8,1]{3,0,2,1:T(8,128)(2,1)S(1)} %get-tuple-element.133), channel_id=1, source_target_pairs={{16,0},{32,16},{48,32},{64,48},{80,64},{96,80},{112,96},{17,1},{33... | collective-permute-start | bytes 12296 | tf_op jit(solution)/shard_map/ppermute | solution.py:18
  74.5 0.9 copy-start.18
  75.7 0.7 copy-start.11
  75.7 2.9 copy-start.9
  77.1 1.0 copy-start.13
  77.2 1.0 copy-start.15
  77.2 1.7 copy-start.7
  77.2 10.4 %copy-start.3 = (bf16[64,2,8,128]{3,0,2,1:T(8,128)(2,1)}, bf16[64,2,8,128]{3,0,2,1:T(8,128)(2,1)S(1)}, u32[]{:S(2)}) copy-start(bf16[64,2,8,128]{3,0,2,1:T(8,128)(2,1)S(1)} %get-tuple-element.120) | copy-start | bytes 786436
  77.2 10.8 %copy-start.5 = (bf16[64,2,8,128]{3,0,2,1:T(8,128)(2,1)}, bf16[64,2,8,128]{3,0,2,1:T(8,128)(2,1)S(1)}, u32[]{:S(2)}) copy-start(bf16[64,2,8,128]{3,0,2,1:T(8,128)(2,1)S(1)} %get-tuple-element.141) | copy-start | bytes 786436
  78.5 1.0 copy-start.23
  92.9 3.9 collective-permute-start.4
  94.9 5.7 %collective-permute-start.5 = (bf16[64,1,8,128]{3,0,2,1:T(8,128)(2,1)S(1)}, bf16[64,1,8,128]{3,0,2,1:T(8,128)(2,1)S(1)}, u32[]{:S(2)}, u32[]{:S(2)}) collective-permute-start(bf16[64,1,8,128]{3,0,2,1:T(8,128)(2,1)S(1)} %get-tuple-element.147), channel_id=1, source_target_pairs={{1,0},{2,1},{3,2},{4,3},{5,4},{6,5},{7,6},{8,7},{9,8},{10,9},{11,1... | collective-permute-start | bytes 393224 | tf_op jit(solution)/shard_map/ppermute | solution.py:18
  96.8 3.8 copy-start.19
  100.6 0.7 copy-start.21
  101.4 7.8 %copy-start.36 = (s32[1,128]{1,0:T(1,128)S(1)}, s32[1,128]{1,0:T(1,128)}, u32[]{:S(2)}) copy-start(s32[1,128]{1,0:T(1,128)} %param.10) | copy-start | bytes 1540
  102.5 10.6 %collective-permute-start.6 = (bf16[64,4,8,1]{3,0,2,1:T(8,128)(2,1)}, bf16[64,4,8,1]{3,0,2,1:T(8,128)(2,1)}, u32[]{:S(2)}, u32[]{:S(2)}) collective-permute-start(bf16[64,4,8,1]{3,0,2,1:T(8,128)(2,1)} %get-tuple-element.130), channel_id=1, source_target_pairs={{0,16},{16,32},{32,48},{48,64},{64,80},{80,96},{96,112},{1,17},{17... | collective-permute-start | bytes 12296 | tf_op jit(solution)/shard_map/ppermute | solution.py:17
  106.7 10.8 %collective-permute-start.7 = (bf16[64,4,8,1]{3,0,2,1:T(8,128)(2,1)}, bf16[64,4,8,1]{3,0,2,1:T(8,128)(2,1)}, u32[]{:S(2)}, u32[]{:S(2)}) collective-permute-start(bf16[64,4,8,1]{3,0,2,1:T(8,128)(2,1)} %get-tuple-element.131), channel_id=1, source_target_pairs={{16,0},{32,16},{48,32},{64,48},{80,64},{96,80},{112,96},{17,1},{33... | collective-permute-start | bytes 12296 | tf_op jit(solution)/shard_map/ppermute | solution.py:18
  120.6 0.9 copy-start.20
  120.6 1.0 copy-start.22
  126.2 1.0 copy-start.25
  139.4 0.7 copy-start.32
  140.9 1.0 copy-start.29
  149.3 7.2 %collective-permute-start.8 = (bf16[64,1,8,128]{3,0,2,1:T(8,128)(2,1)S(1)}, bf16[64,1,8,128]{3,0,2,1:T(8,128)(2,1)S(1)}, u32[]{:S(2)}, u32[]{:S(2)}) collective-permute-start(bf16[64,1,8,128]{3,0,2,1:T(8,128)(2,1)S(1)} %get-tuple-element.144), channel_id=1, source_target_pairs={{0,1},{1,2},{2,3},{3,4},{4,5},{5,6},{6,7},{7,8},{8,9},{9,10},{10,1... | collective-permute-start | bytes 393224 | tf_op jit(solution)/shard_map/ppermute | solution.py:17
  154.5 5.7 %collective-permute-start.9 = (bf16[64,1,8,128]{3,0,2,1:T(8,128)(2,1)S(1)}, bf16[64,1,8,128]{3,0,2,1:T(8,128)(2,1)S(1)}, u32[]{:S(2)}, u32[]{:S(2)}) collective-permute-start(bf16[64,1,8,128]{3,0,2,1:T(8,128)(2,1)S(1)} %get-tuple-element.145), channel_id=1, source_target_pairs={{1,0},{2,1},{3,2},{4,3},{5,4},{6,5},{7,6},{8,7},{9,8},{10,9},{11,1... | collective-permute-start | bytes 393224 | tf_op jit(solution)/shard_map/ppermute | solution.py:18
  160.6 9.9 %collective-permute-start.10 = (bf16[64,4,8,1]{3,0,2,1:T(8,128)(2,1)S(1)}, bf16[64,4,8,1]{3,0,2,1:T(8,128)(2,1)S(1)}, u32[]{:S(2)}, u32[]{:S(2)}) collective-permute-start(bf16[64,4,8,1]{3,0,2,1:T(8,128)(2,1)S(1)} %get-tuple-element.128), channel_id=1, source_target_pairs={{0,16},{16,32},{32,48},{48,64},{64,80},{80,96},{96,112},{1,17},{17... | collective-permute-start | bytes 12296 | tf_op jit(solution)/shard_map/ppermute | solution.py:17
  164.4 10.5 %collective-permute-start.11 = (bf16[64,4,8,1]{3,0,2,1:T(8,128)(2,1)S(1)}, bf16[64,4,8,1]{3,0,2,1:T(8,128)(2,1)S(1)}, u32[]{:S(2)}, u32[]{:S(2)}) collective-permute-start(bf16[64,4,8,1]{3,0,2,1:T(8,128)(2,1)S(1)} %get-tuple-element.129), channel_id=1, source_target_pairs={{16,0},{32,16},{48,32},{64,48},{80,64},{96,80},{112,96},{17,1},{33... | collective-permute-start | bytes 12296 | tf_op jit(solution)/shard_map/ppermute | solution.py:18
  166.6 3.9 copy-start.27
  196.8 1.0 copy-start.12
  196.9 1.2 copy-start.16
  197.1 1.1 copy-start.14
  198.7 1.4 copy-start.10
  199.8 1.0 copy-start.8
  201.5 1.4 copy-start.6
  201.8 1.3 copy-start.4
  203.5 5.4 %collective-permute-start.12 = (bf16[64,1,8,128]{3,0,2,1:T(8,128)(2,1)S(1)}, bf16[64,1,8,128]{3,0,2,1:T(8,128)(2,1)S(1)}, u32[]{:S(2)}, u32[]{:S(2)}) collective-permute-start(bf16[64,1,8,128]{3,0,2,1:T(8,128)(2,1)S(1)} %get-tuple-element.142), channel_id=1, source_target_pairs={{0,1},{1,2},{2,3},{3,4},{4,5},{5,6},{6,7},{7,8},{8,9},{9,10},{10,1... | collective-permute-start | bytes 393224 | tf_op jit(solution)/shard_map/ppermute | solution.py:17
  207.0 5.7 %collective-permute-start.13 = (bf16[64,1,8,128]{3,0,2,1:T(8,128)(2,1)S(1)}, bf16[64,1,8,128]{3,0,2,1:T(8,128)(2,1)S(1)}, u32[]{:S(2)}, u32[]{:S(2)}) collective-permute-start(bf16[64,1,8,128]{3,0,2,1:T(8,128)(2,1)S(1)} %get-tuple-element.143), channel_id=1, source_target_pairs={{1,0},{2,1},{3,2},{4,3},{5,4},{6,5},{7,6},{8,7},{9,8},{10,9},{11,1... | collective-permute-start | bytes 393224 | tf_op jit(solution)/shard_map/ppermute | solution.py:18
  213.0 10.2 %collective-permute-start.14 = (bf16[64,4,8,1]{3,0,2,1:T(8,128)(2,1)S(1)}, bf16[64,4,8,1]{3,0,2,1:T(8,128)(2,1)S(1)}, u32[]{:S(2)}, u32[]{:S(2)}) collective-permute-start(bf16[64,4,8,1]{3,0,2,1:T(8,128)(2,1)S(1)} %get-tuple-element.126), channel_id=1, source_target_pairs={{0,16},{16,32},{32,48},{48,64},{64,80},{80,96},{96,112},{1,17},{17... | collective-permute-start | bytes 12296 | tf_op jit(solution)/shard_map/ppermute | solution.py:17
  217.2 10.5 %collective-permute-start.15 = (bf16[64,4,8,1]{3,0,2,1:T(8,128)(2,1)S(1)}, bf16[64,4,8,1]{3,0,2,1:T(8,128)(2,1)S(1)}, u32[]{:S(2)}, u32[]{:S(2)}) collective-permute-start(bf16[64,4,8,1]{3,0,2,1:T(8,128)(2,1)S(1)} %get-tuple-element.127), channel_id=1, source_target_pairs={{16,0},{32,16},{48,32},{64,48},{80,64},{96,80},{112,96},{17,1},{33... | collective-permute-start | bytes 12296 | tf_op jit(solution)/shard_map/ppermute | solution.py:18
  219.4 8.9 %copy-start.28 = (f32[27,64,64]{2,1,0:T(8,128)}, f32[27,64,64]{2,1,0:T(8,128)S(1)}, u32[]{:S(2)}) copy-start(f32[27,64,64]{2,1,0:T(8,128)S(1)} %fusion.92) | copy-start | bytes 1327108
  228.3 1.3 copy-start.24
  248.6 1.0 copy-start.2
  251.0 0.9 copy-start.35
  252.5 8.4 %copy-start.31 = (bf16[64,256,1]{1,0,2:T(8,128)(2,1)S(1)}, bf16[64,256,1]{1,0,2:T(8,128)(2,1)}, u32[]{:S(2)}) copy-start(bf16[64,256,1]{1,0,2:T(8,128)(2,1)} %copy-done.30) | copy-start | bytes 98308
  253.7 18.3 %all-to-all-start.2 = ((bf16[128,2,512]{2,1,0:T(2,128)(2,1)}), bf16[128,2,512]{2,1,0:T(2,128)(2,1)S(1)}, u32[]{:S(2)}, u32[]{:S(2)}) async-start(bf16[128,2,512]{2,1,0:T(2,128)(2,1)} %reshape.687), calls=%async_computation.2 | async-start | bytes 524288 | tf_op jit(solution)/shard_map/all_to_all | solution.py:127
  260.8 1.0 copy-start.26
  260.8 159.9 %all-reduce.7.cloned.1.call-start = ((), (), s32[]{:S(2)}) async-start(), calls=%async_computation.3 | async-start | bytes 4063232 | tf_op jit(solution)/shard_map/psum | solution.py:129
Sparse Core Ops, SparseCore 0:
  267.6 153.0 all-reduce.6
where the time goes:
time: 441 us; the launch traced here: 432 us
  waiting for transfers between devices  219 us (50%)
  starting transfers between devices  66 us (15%)
  matrix products  65.7 us (15%)
  local copies, waits for them, and re-layouts  41.5 us (9%)
  other arithmetic  23.5 us (5%)
  between operations  16.7 us (4%)
    psum x1, waiting for transfers between devices, local(): lax.psum((term_one, term_two, term_up), ('gz', 'xy'))  147 us
    dot_general x108, matrix products, convolve(): jnp.dot(orient(weights[index], direction), window(padded, offset, directi...  50.1 us
    ppermute x8, waiting for transfers between devices, with_halo(): after = lax.ppermute(first, axis, down)  32.5 us
    ppermute x8, starting transfers between devices, with_halo(): before = lax.ppermute(last, axis, up)  29.5 us
    slice x108, local copies, waits for them, and re-layouts, window(): part = padded[:, 1 + ox:1 + ox + nx, 1 + oy:1 + oy + ny, 1 + oz:1 + oz + nz]  23.1 us
    ppermute x8, waiting for transfers between devices, with_halo(): before = lax.ppermute(last, axis, up)  13.9 us
    ppermute x8, starting transfers between devices, with_halo(): after = lax.ppermute(first, axis, down)  13.4 us
    dot_general x54, matrix products, weight_terms(): lax.dot_general(flat, window(padded, offset, 1, shape), (((1,), (1,)), ((...  13.2 us
  transfers between devices with their start and end apart: 20, of which 20 were waited for; matrix products, arithmetic and copies ran while one was open for 3% of the time, Pallas kernels for 0%

commit v1 on v0

--- a/solution.py
+++ b/solution.py
@@ -3,6 +3,7 @@
 import jax.numpy as jnp
 from jax import lax
 from jax.sharding import PartitionSpec as P
+from jax.lax import psum
 
 OFFSETS = [(a, b, c) for a in (-1, 0, 1) for b in (-1, 0, 1) for c in (-1, 0, 1)]
 
@@ -126,7 +127,7 @@
     ).astype(jnp.bfloat16)
     returned = lax.all_to_all(slot_grad, ("gz", "xy"), split_axis=1, concat_axis=1, tiled=True)
     grad_parent = jnp.where(live[None, :], returned, jnp.zeros_like(returned))[None]
-    sum_one, sum_two, sum_up = lax.psum((term_one, term_two, term_up), ("gz", "xy"))
+    sum_one, sum_two, sum_up = psum(psum((term_one, term_two, term_up), axis_name="gz"), "xy")
     scale = 1.0 / math.sqrt(size_x * count_xy * size_y * size_z * count_gz)
     return (decoded, grad_parent, sum_one * scale, sum_two * scale, sum_up * scale)
 

time: 441 us -> 424 us (0.961)
  the two profiles are of different devices: /device:TPU:1 before, /device:TPU:0 now
where the time goes in v1:
time: 424 us; the launch traced here: 415 us
  waiting for transfers between devices  204 us (48%)
  starting transfers between devices  73.9 us (17%)
  matrix products  65.8 us (16%)
  local copies, waits for them, and re-layouts  36.6 us (9%)
  other arithmetic  18.7 us (4%)
  between operations  16.4 us (4%)
    psum x1, waiting for transfers between devices, local(): psum(psum((term_one, term_two, term_up), axis_name='gz'), 'xy')  73.5 us
    psum x1, waiting for transfers between devices, local(): psum((term_one, term_two, term_up), axis_name='gz')  71.8 us
    dot_general x108, matrix products, convolve(): jnp.dot(orient(weights[index], direction), window(padded, offset, directi...  50.2 us
    ppermute x8, starting transfers between devices, with_halo(): before = lax.ppermute(last, axis, up)  38.7 us
    ppermute x8, waiting for transfers between devices, with_halo(): after = lax.ppermute(first, axis, down)  29 us
    slice x108, local copies, waits for them, and re-layouts, window(): part = padded[:, 1 + ox:1 + ox + nx, 1 + oy:1 + oy + ny, 1 + oz:1 + oz + nz]  23.1 us
    dot_general x54, matrix products, weight_terms(): lax.dot_general(flat, window(padded, offset, 1, shape), (((1,), (1,)), ((...  13.2 us
    all_to_all x1, starting transfers between devices, local(): lax.all_to_all(parent_cell, ('gz', 'xy'), split_axis=1, concat_axis=1, ti...  11.2 us
  transfers between devices with their start and end apart: 21, of which 17 were waited for; matrix products, arithmetic and copies ran while one was open for 3% of the time, Pallas kernels for 0%

profile of v1, /device:TPU:0, one launch (start us, length us, event | category | flops | bytes accessed | tf_op | source)
XLA Modules:
  0.0 415.4 jit_solution(8600361435045094774)
XLA Ops:
  7.7 1.4 reduce.6
  9.8 11.2 %all-to-all-start.1 = ((s32[1,128,16]{2,0,1:T(1,128)}), s32[1,128,16]{2,0,1:T(1,128)S(1)}, u32[]{:S(2)}, u32[]{:S(2)}) async-start(s32[1,128,16]{2,0,1:T(1,128)} %bitcast.3), calls=%async_computation.1 | async-start | bytes 131072 | tf_op jit(solution)/shard_map/all_to_all | solution.py:87
  21.7 1.2 copy.273
  23.3 1.0 reshape.685
  24.3 6.1 %all-to-all-done.1 = s32[1,128,16]{2,0,1:T(1,128)S(1)} async-done(((s32[1,128,16]{2,0,1:T(1,128)}), s32[1,128,16]{2,0,1:T(1,128)S(1)}, u32[]{:S(2)}, u32[]{:S(2)}) %all-to-all-start.1) | async-done | bytes 8224 | tf_op jit(solution)/shard_map/all_to_all | solution.py:87
  30.4 4.6 %all-to-all-start = ((bf16[128,2,512]{2,1,0:T(2,128)(2,1)}), bf16[128,2,512]{2,1,0:T(2,128)(2,1)S(1)}, u32[]{:S(2)}, u32[]{:S(2)}) async-start(bf16[128,2,512]{2,1,0:T(2,128)(2,1)} %reshape.685), calls=%async_computation | async-start | bytes 524288 | tf_op jit(solution)/shard_map/all_to_all | solution.py:86
  36.0 9.9 %all-to-all-done = bf16[128,2,512]{2,1,0:T(2,128)(2,1)S(1)} async-done(((bf16[128,2,512]{2,1,0:T(2,128)(2,1)}), bf16[128,2,512]{2,1,0:T(2,128)(2,1)S(1)}, u32[]{:S(2)}, u32[]{:S(2)}) %all-to-all-start) | async-done | bytes 262176 | tf_op jit(solution)/shard_map/all_to_all | solution.py:86
  48.6 2.7 collective-permute-start
  51.4 1.3 collective-permute-start.1
  54.1 4.2 %collective-permute-done.1 = bf16[64,1,8,128]{3,0,2,1:T(8,128)(2,1)S(1)} collective-permute-done((bf16[64,1,8,128]{3,0,2,1:T(8,128)(2,1)S(1)}, bf16[64,1,8,128]{3,0,2,1:T(8,128)(2,1)S(1)}, u32[]{:S(2)}, u32[]{:S(2)}) %collective-permute-start.1) | collective-permute-done | bytes 131104 | tf_op jit(solution)/shard_map/ppermute | solution.py:19
  58.6 1.3 collective-permute-start.2
  59.9 1.3 collective-permute-start.3
  61.2 1.7 fusion.118
  62.9 1.6 collective-permute-done.3
  65.2 1.3 fusion.605
  71.6 0.9 convolution_bitcast_fusion.11
  72.7 0.9 convolution_bitcast_fusion.12
  83.8 2.3 collective-permute-start.4
  86.0 1.3 collective-permute-start.5
  87.3 1.2 collective-permute-done.4
  88.5 4.4 %collective-permute-done.5 = bf16[64,1,8,128]{3,0,2,1:T(8,128)(2,1)S(1)} collective-permute-done((bf16[64,1,8,128]{3,0,2,1:T(8,128)(2,1)S(1)}, bf16[64,1,8,128]{3,0,2,1:T(8,128)(2,1)S(1)}, u32[]{:S(2)}, u32[]{:S(2)}) %collective-permute-start.5) | collective-permute-done | bytes 131104 | tf_op jit(solution)/shard_map/ppermute | solution.py:19
  93.2 7.7 %collective-permute-start.6 = (bf16[64,4,8,1]{3,0,2,1:T(8,128)(2,1)S(1)}, bf16[64,4,8,1]{3,0,2,1:T(8,128)(2,1)S(1)}, u32[]{:S(2)}, u32[]{:S(2)}) collective-permute-start(bf16[64,4,8,1]{3,0,2,1:T(8,128)(2,1)S(1)} %get-tuple-element.133), channel_id=1, source_target_pairs={{0,16},{16,32},{32,48},{48,64},{64,80},{80,96},{96,112},{1,17},{17... | collective-permute-start | bytes 12296 | tf_op jit(solution)/shard_map/ppermute | solution.py:18
  100.9 1.9 collective-permute-start.7
  102.8 3.6 collective-permute-done.7
  107.1 1.2 fusion.604
  133.3 5.5 %collective-permute-start.8 = (bf16[64,1,8,128]{3,0,2,1:T(8,128)(2,1)S(1)}, bf16[64,1,8,128]{3,0,2,1:T(8,128)(2,1)S(1)}, u32[]{:S(2)}, u32[]{:S(2)}) collective-permute-start(bf16[64,1,8,128]{3,0,2,1:T(8,128)(2,1)S(1)} %get-tuple-element.147), channel_id=1, source_target_pairs={{0,1},{1,2},{2,3},{3,4},{4,5},{5,6},{6,7},{7,8},{8,9},{9,10},{10,1... | collective-permute-start | bytes 393224 | tf_op jit(solution)/shard_map/ppermute | solution.py:18
  138.8 1.3 collective-permute-start.9
  141.3 4.4 %collective-permute-done.9 = bf16[64,1,8,128]{3,0,2,1:T(8,128)(2,1)S(1)} collective-permute-done((bf16[64,1,8,128]{3,0,2,1:T(8,128)(2,1)S(1)}, bf16[64,1,8,128]{3,0,2,1:T(8,128)(2,1)S(1)}, u32[]{:S(2)}, u32[]{:S(2)}) %collective-permute-start.9) | collective-permute-done | bytes 131104 | tf_op jit(solution)/shard_map/ppermute | solution.py:19
  146.0 7.7 %collective-permute-start.10 = (bf16[64,4,8,1]{3,0,2,1:T(8,128)(2,1)S(1)}, bf16[64,4,8,1]{3,0,2,1:T(8,128)(2,1)S(1)}, u32[]{:S(2)}, u32[]{:S(2)}) collective-permute-start(bf16[64,4,8,1]{3,0,2,1:T(8,128)(2,1)S(1)} %get-tuple-element.131), channel_id=1, source_target_pairs={{0,16},{16,32},{32,48},{48,64},{64,80},{80,96},{96,112},{1,17},{17... | collective-permute-start | bytes 12296 | tf_op jit(solution)/shard_map/ppermute | solution.py:18
  153.7 1.3 collective-permute-start.11
  156.2 2.6 collective-permute-done.11
  159.5 1.2 fusion.603
  165.7 1.0 convolution_bitcast_fusion.34
  166.9 1.0 convolution_bitcast_fusion.30
  168.0 1.0 convolution_bitcast_fusion.31
  169.2 1.0 convolution_bitcast_fusion.32
  170.4 1.0 convolution_bitcast_fusion.36
  171.6 1.0 convolution_bitcast_fusion.37
  172.7 1.0 convolution_bitcast_fusion.38
  173.9 1.0 convolution_bitcast_fusion.39
  179.2 1.1 multiply_convert_fusion.1
  187.1 3.8 collective-permute-start.12
  190.9 1.3 collective-permute-start.13
  193.4 4.4 %collective-permute-done.13 = bf16[64,1,8,128]{3,0,2,1:T(8,128)(2,1)S(1)} collective-permute-done((bf16[64,1,8,128]{3,0,2,1:T(8,128)(2,1)S(1)}, bf16[64,1,8,128]{3,0,2,1:T(8,128)(2,1)S(1)}, u32[]{:S(2)}, u32[]{:S(2)}) %collective-permute-start.13) | collective-permute-done | bytes 131104 | tf_op jit(solution)/shard_map/ppermute | solution.py:19
  198.0 7.7 %collective-permute-start.14 = (bf16[64,4,8,1]{3,0,2,1:T(8,128)(2,1)S(1)}, bf16[64,4,8,1]{3,0,2,1:T(8,128)(2,1)S(1)}, u32[]{:S(2)}, u32[]{:S(2)}) collective-permute-start(bf16[64,4,8,1]{3,0,2,1:T(8,128)(2,1)S(1)} %get-tuple-element.129), channel_id=1, source_target_pairs={{0,16},{16,32},{32,48},{48,64},{64,80},{80,96},{96,112},{1,17},{17... | collective-permute-start | bytes 12296 | tf_op jit(solution)/shard_map/ppermute | solution.py:18
  205.8 1.3 collective-permute-start.15
  207.4 3.9 collective-permute-done.15
  211.9 1.1 fusion.602
  221.6 1.0 convolution_bitcast_fusion.24
  222.8 1.0 convolution_bitcast_fusion.20
  223.9 1.0 convolution_bitcast_fusion.21
  225.1 1.0 convolution_bitcast_fusion.22
  226.3 1.0 convolution_bitcast_fusion.26
  227.4 1.0 convolution_bitcast_fusion.27
  228.6 1.0 convolution_bitcast_fusion.28
  229.8 1.0 convolution_bitcast_fusion.29
  232.5 1.4 fusion.121
  235.7 71.8 %all-reduce.11.cloned.1.call-done = (f32[27,64,64]{2,1,0:T(8,128)}, f32[27,64,64]{2,1,0:T(8,128)}, f32[8,64,64]{2,1,0:T(8,128)}) async-done(((f32[27,64,64]{2,1,0:T(8,128)}, f32[27,64,64]{2,1,0:T(8,128)}, f32[8,64,64]{2,1,0:T(8,128)}), (f32[27,64,64]{2,1,0:T(8,128)}, f32[27,64,64]{2,1,0:T(8,128)}, f32[8,64,64]{2,1,0:T(8,128)})) %all-reduce.11.cloned.1.call-update) | async-done | bytes 1015824 | tf_op jit(solution)/shard_map/psum | solution.py:130
  308.5 1.0 reshape.687
  309.5 8.4 %all-to-all-start.2 = ((bf16[128,2,512]{2,1,0:T(2,128)(2,1)}), bf16[128,2,512]{2,1,0:T(2,128)(2,1)S(1)}, u32[]{:S(2)}, u32[]{:S(2)}) async-start(bf16[128,2,512]{2,1,0:T(2,128)(2,1)} %reshape.687), calls=%async_computation.2 | async-start | bytes 524288 | tf_op jit(solution)/shard_map/all_to_all | solution.py:128
  318.9 9.8 %all-to-all-done.2 = bf16[128,2,512]{2,1,0:T(2,128)(2,1)S(1)} async-done(((bf16[128,2,512]{2,1,0:T(2,128)(2,1)}), bf16[128,2,512]{2,1,0:T(2,128)(2,1)S(1)}, u32[]{:S(2)}, u32[]{:S(2)}) %all-to-all-start.2) | async-done | bytes 262176 | tf_op jit(solution)/shard_map/all_to_all | solution.py:128
  330.3 73.5 %all-reduce.9.cloned.1.call-done = (f32[27,64,64]{2,1,0:T(8,128)}, f32[27,64,64]{2,1,0:T(8,128)}, f32[8,64,64]{2,1,0:T(8,128)}) async-done(((f32[27,64,64]{2,1,0:T(8,128)}, f32[27,64,64]{2,1,0:T(8,128)}, f32[8,64,64]{2,1,0:T(8,128)}), (f32[27,64,64]{2,1,0:T(8,128)}, f32[27,64,64]{2,1,0:T(8,128)}, f32[8,64,64]{2,1,0:T(8,128)})) %all-reduce.9.cloned.1.call-update) | async-done | bytes 1015824 | tf_op jit(solution)/shard_map/psum | solution.py:130
  403.8 1.7 broadcast_multiply_fusion.2
  405.5 2.9 broadcast_multiply_fusion
  (334 shorter events, 88.2 us)
Async XLA Ops:
  7.2 39.7 %copy-start = (bf16[8,64,64]{2,1,0:T(8,128)(2,1)S(1)}, bf16[8,64,64]{2,1,0:T(8,128)(2,1)}, u32[]{:S(2)}) copy-start(bf16[8,64,64]{2,1,0:T(8,128)(2,1)} %param.11) | copy-start | bytes 196612
  9.8 20.6 %all-to-all-start.1 = ((s32[1,128,16]{2,0,1:T(1,128)}), s32[1,128,16]{2,0,1:T(1,128)S(1)}, u32[]{:S(2)}, u32[]{:S(2)}) async-start(s32[1,128,16]{2,0,1:T(1,128)} %bitcast.3), calls=%async_computation.1 | async-start | bytes 131072 | tf_op jit(solution)/shard_map/all_to_all | solution.py:87
  22.9 12.1 %copy-start.6 = (s32[2,8,128]{2,1,0:T(8,128)S(1)}, s32[2,8,128]{2,1,0:T(8,128)}, u32[]{:S(2)}) copy-start(s32[2,8,128]{2,1,0:T(8,128)} %param.14) | copy-start | bytes 24580
  30.4 15.5 %all-to-all-start = ((bf16[128,2,512]{2,1,0:T(2,128)(2,1)}), bf16[128,2,512]{2,1,0:T(2,128)(2,1)S(1)}, u32[]{:S(2)}, u32[]{:S(2)}) async-start(bf16[128,2,512]{2,1,0:T(2,128)(2,1)} %reshape.685), calls=%async_computation | async-start | bytes 524288 | tf_op jit(solution)/shard_map/all_to_all | solution.py:86
  35.0 272.5 %all-reduce.11.cloned.1.call-start = ((), (), s32[]{:S(2)}) async-start(), calls=%async_computation.4 | async-start | bytes 4063232 | tf_op jit(solution)/shard_map/psum | solution.py:130
  48.6 5.4 %collective-permute-start = (bf16[64,1,8,128]{3,0,2,1:T(8,128)(2,1)S(1)}, bf16[64,1,8,128]{3,0,2,1:T(8,128)(2,1)S(1)}, u32[]{:S(2)}, u32[]{:S(2)}) collective-permute-start(bf16[64,1,8,128]{3,0,2,1:T(8,128)(2,1)S(1)} %get-tuple-element.151), channel_id=1, source_target_pairs={{0,1},{1,2},{2,3},{3,4},{4,5},{5,6},{6,7},{7,8},{8,9},{9,10},{10,1... | collective-permute-start | bytes 393224 | tf_op jit(solution)/shard_map/ppermute | solution.py:18
  51.4 6.9 %collective-permute-start.1 = (bf16[64,1,8,128]{3,0,2,1:T(8,128)(2,1)S(1)}, bf16[64,1,8,128]{3,0,2,1:T(8,128)(2,1)S(1)}, u32[]{:S(2)}, u32[]{:S(2)}) collective-permute-start(bf16[64,1,8,128]{3,0,2,1:T(8,128)(2,1)S(1)} %get-tuple-element.152), channel_id=1, source_target_pairs={{1,0},{2,1},{3,2},{4,3},{5,4},{6,5},{7,6},{8,7},{9,8},{10,9},{11,1... | collective-permute-start | bytes 393224 | tf_op jit(solution)/shard_map/ppermute | solution.py:19
  58.6 4.3 %collective-permute-start.2 = (bf16[64,4,8,1]{3,0,2,1:T(8,128)(2,1)S(1)}, bf16[64,4,8,1]{3,0,2,1:T(8,128)(2,1)S(1)}, u32[]{:S(2)}, u32[]{:S(2)}) collective-permute-start(bf16[64,4,8,1]{3,0,2,1:T(8,128)(2,1)S(1)} %get-tuple-element.135), channel_id=1, source_target_pairs={{0,16},{16,32},{32,48},{48,64},{64,80},{80,96},{96,112},{1,17},{17... | collective-permute-start | bytes 12296 | tf_op jit(solution)/shard_map/ppermute | solution.py:18
  59.9 4.6 %collective-permute-start.3 = (bf16[64,4,8,1]{3,0,2,1:T(8,128)(2,1)S(1)}, bf16[64,4,8,1]{3,0,2,1:T(8,128)(2,1)S(1)}, u32[]{:S(2)}, u32[]{:S(2)}) collective-permute-start(bf16[64,4,8,1]{3,0,2,1:T(8,128)(2,1)S(1)} %get-tuple-element.136), channel_id=1, source_target_pairs={{16,0},{32,16},{48,32},{64,48},{80,64},{96,80},{112,96},{17,1},{33... | collective-permute-start | bytes 12296 | tf_op jit(solution)/shard_map/ppermute | solution.py:19
  69.3 1.0 copy-start.1
  83.8 4.8 %collective-permute-start.4 = (bf16[64,1,8,128]{3,0,2,1:T(8,128)(2,1)S(1)}, bf16[64,1,8,128]{3,0,2,1:T(8,128)(2,1)S(1)}, u32[]{:S(2)}, u32[]{:S(2)}) collective-permute-start(bf16[64,1,8,128]{3,0,2,1:T(8,128)(2,1)S(1)} %get-tuple-element.149), channel_id=1, source_target_pairs={{0,1},{1,2},{2,3},{3,4},{4,5},{5,6},{6,7},{7,8},{8,9},{9,10},{10,1... | collective-permute-start | bytes 393224 | tf_op jit(solution)/shard_map/ppermute | solution.py:18
  86.0 6.9 %collective-permute-start.5 = (bf16[64,1,8,128]{3,0,2,1:T(8,128)(2,1)S(1)}, bf16[64,1,8,128]{3,0,2,1:T(8,128)(2,1)S(1)}, u32[]{:S(2)}, u32[]{:S(2)}) collective-permute-start(bf16[64,1,8,128]{3,0,2,1:T(8,128)(2,1)S(1)} %get-tuple-element.150), channel_id=1, source_target_pairs={{1,0},{2,1},{3,2},{4,3},{5,4},{6,5},{7,6},{8,7},{9,8},{10,9},{11,1... | collective-permute-start | bytes 393224 | tf_op jit(solution)/shard_map/ppermute | solution.py:19
  93.2 9.6 %collective-permute-start.6 = (bf16[64,4,8,1]{3,0,2,1:T(8,128)(2,1)S(1)}, bf16[64,4,8,1]{3,0,2,1:T(8,128)(2,1)S(1)}, u32[]{:S(2)}, u32[]{:S(2)}) collective-permute-start(bf16[64,4,8,1]{3,0,2,1:T(8,128)(2,1)S(1)} %get-tuple-element.133), channel_id=1, source_target_pairs={{0,16},{16,32},{32,48},{48,64},{64,80},{80,96},{96,112},{1,17},{17... | collective-permute-start | bytes 12296 | tf_op jit(solution)/shard_map/ppermute | solution.py:18
  100.9 5.5 %collective-permute-start.7 = (bf16[64,4,8,1]{3,0,2,1:T(8,128)(2,1)S(1)}, bf16[64,4,8,1]{3,0,2,1:T(8,128)(2,1)S(1)}, u32[]{:S(2)}, u32[]{:S(2)}) collective-permute-start(bf16[64,4,8,1]{3,0,2,1:T(8,128)(2,1)S(1)} %get-tuple-element.134), channel_id=1, source_target_pairs={{16,0},{32,16},{48,32},{64,48},{80,64},{96,80},{112,96},{17,1},{33... | collective-permute-start | bytes 12296 | tf_op jit(solution)/shard_map/ppermute | solution.py:19
  111.2 1.0 copy-start.2
  125.6 1.0 copy-start.5
  133.3 8.0 %collective-permute-start.8 = (bf16[64,1,8,128]{3,0,2,1:T(8,128)(2,1)S(1)}, bf16[64,1,8,128]{3,0,2,1:T(8,128)(2,1)S(1)}, u32[]{:S(2)}, u32[]{:S(2)}) collective-permute-start(bf16[64,1,8,128]{3,0,2,1:T(8,128)(2,1)S(1)} %get-tuple-element.147), channel_id=1, source_target_pairs={{0,1},{1,2},{2,3},{3,4},{4,5},{5,6},{6,7},{7,8},{8,9},{9,10},{10,1... | collective-permute-start | bytes 393224 | tf_op jit(solution)/shard_map/ppermute | solution.py:18
  138.8 6.9 %collective-permute-start.9 = (bf16[64,1,8,128]{3,0,2,1:T(8,128)(2,1)S(1)}, bf16[64,1,8,128]{3,0,2,1:T(8,128)(2,1)S(1)}, u32[]{:S(2)}, u32[]{:S(2)}) collective-permute-start(bf16[64,1,8,128]{3,0,2,1:T(8,128)(2,1)S(1)} %get-tuple-element.148), channel_id=1, source_target_pairs={{1,0},{2,1},{3,2},{4,3},{5,4},{6,5},{7,6},{8,7},{9,8},{10,9},{11,1... | collective-permute-start | bytes 393224 | tf_op jit(solution)/shard_map/ppermute | solution.py:19
  146.0 9.5 %collective-permute-start.10 = (bf16[64,4,8,1]{3,0,2,1:T(8,128)(2,1)S(1)}, bf16[64,4,8,1]{3,0,2,1:T(8,128)(2,1)S(1)}, u32[]{:S(2)}, u32[]{:S(2)}) collective-permute-start(bf16[64,4,8,1]{3,0,2,1:T(8,128)(2,1)S(1)} %get-tuple-element.131), channel_id=1, source_target_pairs={{0,16},{16,32},{32,48},{48,64},{64,80},{80,96},{96,112},{1,17},{17... | collective-permute-start | bytes 12296 | tf_op jit(solution)/shard_map/ppermute | solution.py:18
  153.7 5.2 %collective-permute-start.11 = (bf16[64,4,8,1]{3,0,2,1:T(8,128)(2,1)S(1)}, bf16[64,4,8,1]{3,0,2,1:T(8,128)(2,1)S(1)}, u32[]{:S(2)}, u32[]{:S(2)}) collective-permute-start(bf16[64,4,8,1]{3,0,2,1:T(8,128)(2,1)S(1)} %get-tuple-element.132), channel_id=1, source_target_pairs={{16,0},{32,16},{48,32},{64,48},{80,64},{96,80},{112,96},{17,1},{33... | collective-permute-start | bytes 12296 | tf_op jit(solution)/shard_map/ppermute | solution.py:19
  155.3 0.9 copy-start.3
  187.1 6.3 %collective-permute-start.12 = (bf16[64,1,8,128]{3,0,2,1:T(8,128)(2,1)S(1)}, bf16[64,1,8,128]{3,0,2,1:T(8,128)(2,1)S(1)}, u32[]{:S(2)}, u32[]{:S(2)}) collective-permute-start(bf16[64,1,8,128]{3,0,2,1:T(8,128)(2,1)S(1)} %get-tuple-element.145), channel_id=1, source_target_pairs={{0,1},{1,2},{2,3},{3,4},{4,5},{5,6},{6,7},{7,8},{8,9},{9,10},{10,1... | collective-permute-start | bytes 393224 | tf_op jit(solution)/shard_map/ppermute | solution.py:18
  190.9 6.9 %collective-permute-start.13 = (bf16[64,1,8,128]{3,0,2,1:T(8,128)(2,1)S(1)}, bf16[64,1,8,128]{3,0,2,1:T(8,128)(2,1)S(1)}, u32[]{:S(2)}, u32[]{:S(2)}) collective-permute-start(bf16[64,1,8,128]{3,0,2,1:T(8,128)(2,1)S(1)} %get-tuple-element.146), channel_id=1, source_target_pairs={{1,0},{2,1},{3,2},{4,3},{5,4},{6,5},{7,6},{8,7},{9,8},{10,9},{11,1... | collective-permute-start | bytes 393224 | tf_op jit(solution)/shard_map/ppermute | solution.py:19
  198.0 9.3 %collective-permute-start.14 = (bf16[64,4,8,1]{3,0,2,1:T(8,128)(2,1)S(1)}, bf16[64,4,8,1]{3,0,2,1:T(8,128)(2,1)S(1)}, u32[]{:S(2)}, u32[]{:S(2)}) collective-permute-start(bf16[64,4,8,1]{3,0,2,1:T(8,128)(2,1)S(1)} %get-tuple-element.129), channel_id=1, source_target_pairs={{0,16},{16,32},{32,48},{48,64},{64,80},{80,96},{96,112},{1,17},{17... | collective-permute-start | bytes 12296 | tf_op jit(solution)/shard_map/ppermute | solution.py:18
  205.8 5.5 %collective-permute-start.15 = (bf16[64,4,8,1]{3,0,2,1:T(8,128)(2,1)S(1)}, bf16[64,4,8,1]{3,0,2,1:T(8,128)(2,1)S(1)}, u32[]{:S(2)}, u32[]{:S(2)}) collective-permute-start(bf16[64,4,8,1]{3,0,2,1:T(8,128)(2,1)S(1)} %get-tuple-element.130), channel_id=1, source_target_pairs={{16,0},{32,16},{48,32},{64,48},{80,64},{96,80},{112,96},{17,1},{33... | collective-permute-start | bytes 12296 | tf_op jit(solution)/shard_map/ppermute | solution.py:19
  207.3 3.9 copy-start.4
  235.7 168.1 %all-reduce.9.cloned.1.call-start = ((), (), s32[]{:S(2)}) async-start(), calls=%async_computation.3 | async-start | bytes 4063232 | tf_op jit(solution)/shard_map/psum | solution.py:130
  308.2 9.7 %copy-start.7 = (s32[1,128]{1,0:T(1,128)S(1)}, s32[1,128]{1,0:T(1,128)}, u32[]{:S(2)}) copy-start(s32[1,128]{1,0:T(1,128)} %param.10) | copy-start | bytes 1540
  309.5 19.2 %all-to-all-start.2 = ((bf16[128,2,512]{2,1,0:T(2,128)(2,1)}), bf16[128,2,512]{2,1,0:T(2,128)(2,1)S(1)}, u32[]{:S(2)}, u32[]{:S(2)}) async-start(bf16[128,2,512]{2,1,0:T(2,128)(2,1)} %reshape.687), calls=%async_computation.2 | async-start | bytes 524288 | tf_op jit(solution)/shard_map/all_to_all | solution.py:128
Sparse Core Ops, SparseCore 0:
  235.8 71.6 all-reduce.10
  311.3 92.5 all-reduce.8
